TPU v7x, 32 devices: a whole 2x2x4 slice. The times are simulated.
32 devices in a mesh: seq: 8 (over z, x), tp: 4 (over y, core).
Axes of the slice: x: 2, y: 2, z: 4, core: 2. Of those that a mesh axis runs over, the one named last changes fastest.
Arguments:
- inner_x: bfloat16 [4, 1024, 8192], P(None, 'seq', 'tp'), may hold values from -6 to 6
- inner_z: bfloat16 [4, 1024, 8192], P(None, 'seq', 'tp'), may hold values from -6 to 6
- conv_tail: bfloat16 [4, 3, 8192], P(None, None, 'tp'), may hold values from -6 to 6
- conv_weight: float32 [4, 8192], P(None, 'tp'), may hold values from -3 to 3
- conv_bias: float32 [8192], P('tp'), may hold values from -3 to 3
- xproj_dt: bfloat16 [8192, 512], P('tp'), may hold values from -0.0625 to 0.0625
- xproj_bc: bfloat16 [8192, 32], P('tp'), may hold values from -0.0625 to 0.0625
- dt_weight: bfloat16 [512, 8192], P(None, 'tp'), may hold values from -0.25 to 0.25
- dt_bias: float32 [8192], P('tp'), may hold values from -5 to -4
- decay_log: float32 [16, 8192], P(None, 'tp'), may hold values from -8 to 1.1
- skip_gain: float32 [8192], P('tp'), may hold values from 0.5 to 1.5
- out_weight: bfloat16 [8192, 8192], P('tp'), may hold values from -0.0625 to 0.0625
- residual: bfloat16 [4, 1024, 8192], P(None, 'seq', 'tp'), may hold values from -6 to 6
- init_state: float32 [4, 16, 8192], P(None, None, 'tp'), may hold values from -6 to 6
Outputs:
- hidden_out: bfloat16 [4, 1024, 8192], P(None, 'seq', 'tp')
- block_states: float32 [8, 4, 16, 8192], P('seq', None, None, 'tp')
All inputs are finite; a program needn't handle non-finite values.
Results may differ from a plain program's by a relative error of at most 0.024.
Values may be sent and summed in bfloat16 or wider, within the bound.
No kernel may reach another device: no remote copies, remote signals or barrier semaphores. Data moves between devices by JAX's collectives and lax.ppermute only.
A program may use at most 128 MiB of HBM per device.

v0:
```python
import jax
import jax.numpy as jnp
from jax import lax
from jax.sharding import PartitionSpec as P


def passed_along(block, axis, distance):
    devices = range(lax.axis_size(axis))
    route = [(i - distance, i) for i in devices if i - distance in devices]
    return lax.ppermute(block, axis, route)


def carried_in(x, axis, join, neutral):
    place = lax.axis_index(axis)
    gathered = jax.tree.map(
        lambda a, kind: lax.all_gather(a.astype(kind), axis), x, (jnp.bfloat16, jnp.bfloat16)
    )
    state = jax.tree.map(lambda a, e: jnp.zeros_like(a) + jnp.asarray(e, a.dtype), x, neutral)

    def one(lap, state):
        return join(
            state,
            jax.tree.map(
                lambda a, own: lax.dynamic_index_in_dim(a, lap, 0, False).astype(own.dtype),
                gathered,
                x,
            ),
        )

    return lax.fori_loop(0, place, one, state)


def run_chain(initial, decay_rates, steps_dt, inputs_x, gates_b, reads_c):

    def advance(carried, packed):
        step_dt, value_x, gate_b, read_c = packed
        factor = jnp.exp(decay_rates[None, :, :] * step_dt[:, None, :])
        carried = factor * carried + (step_dt * value_x)[:, None, :] * gate_b[:, :, None]
        emitted = jnp.sum(read_c[:, :, None] * carried, axis=1)
        return (carried, emitted)

    return lax.scan(advance, initial, (steps_dt, inputs_x, gates_b, reads_c), unroll=8)


def compose(earlier_pair, later_pair):
    return (earlier_pair[0] * later_pair[0], later_pair[0] * earlier_pair[1] + later_pair[1])


def body(
    inner_x,
    inner_z,
    conv_tail,
    conv_weight,
    conv_bias,
    xproj_dt,
    xproj_bc,
    dt_weight,
    dt_bias,
    decay_log,
    skip_gain,
    out_weight,
    residual,
    init_state,
):
    kernel = conv_weight.shape[0]
    length = inner_x.shape[1]
    rim_tokens = inner_x[:, length - (kernel - 1) :, :]
    arrived = passed_along(rim_tokens, "seq", 1)
    earlier = jnp.where(lax.axis_index("seq") == 0, conv_tail, arrived)
    joined = jnp.concatenate([earlier, inner_x], axis=1).astype(jnp.float32)
    conv_mixed = conv_bias + conv_weight[0] * joined[:, 0:length, :]
    for offset in range(1, kernel):
        conv_mixed = conv_mixed + conv_weight[offset] * joined[:, offset : offset + length, :]
    conv_act = jax.nn.silu(conv_mixed).astype(jnp.bfloat16)
    low_part = jnp.dot(conv_act, xproj_dt, preferred_element_type=jnp.float32)
    bc_part = jnp.dot(conv_act, xproj_bc, preferred_element_type=jnp.float32)
    low_rank, bc_proj = (
        lax.psum(low_part.astype(jnp.bfloat16), "tp").astype(jnp.float32),
        lax.psum(bc_part.astype(jnp.bfloat16), "tp").astype(jnp.float32),
    )
    normed = (
        low_rank * lax.rsqrt(jnp.mean(low_rank * low_rank, axis=-1, keepdims=True) + 1e-06)
    ).astype(jnp.bfloat16)
    steps_dt = jax.nn.softplus(
        jnp.dot(normed, dt_weight, preferred_element_type=jnp.float32) + dt_bias
    )
    states_n = init_state.shape[1]
    gates_b = bc_proj[..., :states_n]
    reads_c = bc_proj[..., states_n:]
    decay_rates = -jnp.exp(decay_log)
    values = conv_act.astype(jnp.float32)
    flipped = [
        jnp.transpose(array_in, (1, 0, 2)) for array_in in (steps_dt, values, gates_b, reads_c)
    ]
    zeros_state = jnp.zeros_like(init_state)
    ones_state = jnp.ones_like(init_state)
    local_end, local_out = run_chain(
        zeros_state, decay_rates, flipped[0], flipped[1], flipped[2], flipped[3]
    )
    elapsed = jnp.sum(steps_dt, axis=1)
    through = jnp.exp(decay_rates[None, :, :] * elapsed[:, None, :])
    prior_decay, prior_state = carried_in(
        (through, local_end), "seq", compose, (ones_state, zeros_state)
    )
    entering = prior_decay * init_state + prior_state
    final_state, emitted = run_chain(
        entering, decay_rates, flipped[0], flipped[1], flipped[2], flipped[3]
    )
    scanned = jnp.transpose(emitted, (1, 0, 2)) + skip_gain * values
    gated_out = (scanned * jax.nn.silu(inner_z.astype(jnp.float32))).astype(jnp.bfloat16)
    flat_rows = gated_out.reshape(-1, gated_out.shape[2])
    own_rows = lax.psum_scatter(
        lax.dot_general(
            out_weight, flat_rows, (((0,), (1,)), ((), ())), preferred_element_type=jnp.float32
        ).astype(jnp.bfloat16),
        "tp",
        scatter_dimension=0,
        tiled=True,
    ).astype(jnp.float32)
    summed = jnp.transpose(own_rows).reshape(gated_out.shape[0], gated_out.shape[1], -1)
    hidden_out = (residual.astype(jnp.float32) + summed).astype(jnp.bfloat16)
    return (hidden_out, final_state[None])


def solution(mesh):
    return jax.shard_map(
        body,
        mesh=mesh,
        in_specs=(
            P(None, "seq", "tp"),
            P(None, "seq", "tp"),
            P(None, None, "tp"),
            P(None, "tp"),
            P("tp"),
            P("tp", None),
            P("tp", None),
            P(None, "tp"),
            P("tp"),
            P(None, "tp"),
            P("tp"),
            P("tp", None),
            P(None, "seq", "tp"),
            P(None, None, "tp"),
        ),
        out_specs=(P(None, "seq", "tp"), P("seq", None, None, "tp")),
        check_vma=False,
    )
```

profile of v0, /device:TPU:0, one launch (start us, length us, event | category | flops | bytes accessed | tf_op | source)
XLA Modules:
  0.0 397.8 jit_solution(7436567951743323637)
XLA Ops:
  7.2 1.1 slice.258
  8.4 4.9 %collective-permute-start = (bf16[4,3,2048]{2,0,1:T(4,128)(2,1)S(1)}, bf16[4,3,2048]{2,0,1:T(4,128)(2,1)S(1)}, u32[]{:S(2)}, u32[]{:S(2)}) collective-permute-start(bf16[4,3,2048]{2,0,1:T(4,128)(2,1)S(1)} %copy.48), channel_id=1, source_target_pairs={{0,4},{4,8},{8,12},{12,16},{16,20},{20,24},{24,28},{1,5},{5,9},{9,... | collective-permute-start | bytes 147464 | tf_op jit(solution)/shard_map/ppermute | solution.py:10
  16.1 2.3 maximum_convert_fusion
  18.4 4.2 %convert_bitcast_fusion = (f32[128,4,2048]{2,0,1:T(8,128)}, bf16[4,128,2048]{2,1,0:T(8,128)(2,1)S(1)}) fusion(f32[4,131,2048]{2,1,0:T(8,128)S(1)} %maximum_convert_fusion, f32[2048]{0:T(1024)S(1)} %bitcast.340, f32[2048]{0:T(1024)S(1)} %bitcast.341, f32[2048]{0:T(1024)S(1)} %bitcast.339, f32[2048]{0:T(1024)S(1)} %bitcast.338, f32[2048]{0:T(1024)S(1)} %copy-done.8), kind=kLoop, calls=%fused_computation.138 | loop fusion | flops 14680064 | bytes 23109632 | tf_op jit(solution)/shard_map/transpose | solution.py:93
  22.5 1.3 copy-done.3
  23.8 2.0 fusion.68
  26.0 2.3 convolution_convert_fusion.1
  28.3 10.8 %psum.15 = bf16[4,128,32]{1,2,0:T(8,128)(2,1)S(1)} all-reduce(bf16[4,128,32]{1,2,0:T(8,128)(2,1)S(1)} %convolution_convert_fusion.1), channel_id=1, replica_groups=mesh['seq'=8,'tp'=4] {'tp'}, use_global_device_ids=true, to_apply=%region_3.4 | all-reduce | flops 16384 | bytes 65536 | tf_op jit(solution)/shard_map/psum | solution.py:79
  39.5 6.8 %copy.38 = f32[128,4,2048]{2,1,0:T(4,128)} copy(f32[128,4,2048]{2,0,1:T(8,128)} %get-tuple-element.229) | data formatting | bytes 8388608 | tf_op jit(solution)/shard_map/transpose | solution.py:93
  46.3 14.3 %all-reduce.2.cloned.1.call-done = bf16[4,128,512]{2,1,0:T(8,128)(2,1)} async-done(((bf16[4,128,512]{2,1,0:T(8,128)(2,1)}), bf16[4,128,512]{2,1,0:T(8,128)(2,1)}) %all-reduce.2.cloned.1.call-update) | async-done | bytes 524304 | tf_op jit(solution)/shard_map/psum | solution.py:78
  60.7 1.2 fusion.71
  61.9 2.5 fusion.73
  64.5 4.3 %fusion.55 = f32[16,8,4,2048]{3,1,0,2:T(8,128)} fusion(f32[4,128,2048]{2,1,0:T(8,128)S(1)} %get-tuple-element.296, f32[2048]{0:T(1024)S(1)} %copy-done.7), kind=kLoop, calls=%fused_computation.145 | loop fusion | flops 7340032 | bytes 8396800 | tf_op jit(solution)/shard_map/reshape | solution.py:42
  68.7 2.7 select_reduce_fusion
  72.5 7.0 %copy.40 = f32[16,8,4,2048]{3,2,1,0:T(4,128)} copy(f32[16,8,4,2048]{3,1,0,2:T(8,128)} %fusion.55) | data formatting | bytes 8388608
  79.5 49.1 %while.37 = (s32[]{:T(128)}, f32[4,16,2048]{2,1,0:T(8,128)S(1)}, f32[16,2048]{1,0:T(8,128)S(1)}, f32[16,8,4,2048]{3,2,1,0:T(4,128)}, f32[16,8,4,2048]{3,2,1,0:T(...) while((s32[]{:T(128)}, f32[4,16,2048]{2,1,0:T(8,128)S(1)}, ...), condition=%wide.region_5.6_spmd.clone, body=%wide.region_4.5_spmd.clone.sunk | while | flops 4390922 | bytes 3021131 | solution.py:42
  79.5 1.1 fusion.92
  82.6 1.1 fusion.92
  85.6 1.1 fusion.92
  88.7 1.1 fusion.92
  91.8 1.1 fusion.92
  94.8 1.1 fusion.92
  97.9 1.1 fusion.92
  101.0 1.1 fusion.92
  104.1 1.1 fusion.92
  107.1 1.1 fusion.92
  110.2 1.1 fusion.92
  113.3 1.1 fusion.92
  116.3 1.1 fusion.92
  119.4 1.1 fusion.92
  122.5 1.1 fusion.92
  125.5 1.1 fusion.92
  129.6 49.1 %all-gather.6.cloned.1.call-done = bf16[32,16,2048]{2,1,0:T(8,128)(2,1)} async-done(((bf16[4,16,2048]{2,1,0:T(8,128)(2,1)}), bf16[32,16,2048]{2,1,0:T(8,128)(2,1)}) %all-gather.6.cloned.1.call-update) | async-done | bytes 2097168 | tf_op jit(solution)/shard_map/all_gather | solution.py:16
  179.8 94.4 %while.36 = (s32[]{:T(128)}, f32[4,16,2048]{2,1,0:T(8,128)S(1)}, f32[16,8,4,2048]{3,2,1,0:T(4,128)}, f32[16,2048]{1,0:T(8,128)S(1)}, f32[16,8,4,2048]{3,2,1,0:T(...) while((s32[]{:T(128)}, f32[4,16,2048]{2,1,0:T(8,128)S(1)}, ...), condition=%wide.region_17.18_spmd, body=%wide.region_8.17_spmd.sunk | while | flops 9437193 | bytes 6568305 | solution.py:42
  179.8 1.1 fusion.90
  182.8 1.1 multiply_reduce_fusion.11
  185.8 1.1 fusion.90
  188.7 1.1 multiply_reduce_fusion.11
  191.7 1.1 fusion.90
  194.6 1.1 multiply_reduce_fusion.11
  197.6 1.1 fusion.90
  200.5 1.1 multiply_reduce_fusion.11
  206.4 1.1 multiply_reduce_fusion.11
  209.4 1.1 fusion.90
  212.3 1.1 multiply_reduce_fusion.11
  218.2 1.1 multiply_reduce_fusion.11
  221.2 1.1 fusion.90
  224.1 1.1 multiply_reduce_fusion.11
  230.0 1.1 multiply_reduce_fusion.11
  235.9 1.1 multiply_reduce_fusion.11
  238.9 1.1 fusion.90
  241.9 1.1 multiply_reduce_fusion.11
  244.8 1.1 fusion.90
  247.8 1.1 multiply_reduce_fusion.11
  250.7 1.1 fusion.90
  253.7 1.1 multiply_reduce_fusion.11
  259.5 1.1 multiply_reduce_fusion.11
  265.4 1.1 multiply_reduce_fusion.11
  271.3 1.1 multiply_reduce_fusion.11
  274.3 8.1 %fusion.51 = bf16[4,128,2048]{2,1,0:T(8,128)(2,1)} fusion(bf16[4,128,2048]{2,1,0:T(8,128)(2,1)} %copy-done.3, bf16[4,128,2048]{2,1,0:T(8,128)(2,1)} %param.21, f32[128,4,2048]{2,1,0:T(4,128)} %bitcast.325, f32[2048]{0:T(1024)S(1)} %copy-done.9), kind=kLoop, calls=%fused_computation.141 | loop fusion | flops 10485760 | bytes 10493952 | tf_op jit(solution)/shard_map/convert_element_type | solution.py:110
  282.4 26.0 %fusion.48 = bf16[8192,512]{0,1:T(8,128)(2,1)} fusion(bf16[512,2048]{1,0:T(8,128)(2,1)} %bitcast.326, bf16[2048,8192]{1,0:T(8,128)(2,1)} %param.31), kind=kOutput, calls=%fused_computation.134 | convolution fusion | flops 17184063488 | bytes 44040192 | tf_op jit(solution)/shard_map/dot_general | solution.py:113
  308.4 78.5 %reduce-scatter.2.cloned.1.call-done = bf16[2048,512]{0,1:T(8,128)(2,1)} async-done(((bf16[8192,512]{0,1:T(8,128)(2,1)}), bf16[2048,512]{0,1:T(8,128)(2,1)}) %reduce-scatter.2.cloned.1.call-update) | async-done | bytes 2097168 | tf_op jit(solution)/shard_map/reduce_scatter | solution.py:112
  386.9 2.3 reshape.387
  389.2 2.1 add_convert_fusion
  (329 shorter events, 102.9 us)
Async XLA Ops:
  7.2 54.7 %copy-start = (bf16[512,2048]{1,0:T(8,128)(2,1)S(1)}, bf16[512,2048]{1,0:T(8,128)(2,1)}, u32[]{:S(2)}) copy-start(bf16[512,2048]{1,0:T(8,128)(2,1)} %param.27) | copy-start | bytes 6291460
  7.2 11.2 %copy-start.8 = (f32[2048]{0:T(1024)S(1)}, f32[2048]{0:T(1024)}, u32[]{:S(2)}) copy-start(f32[2048]{0:T(1024)} %param.24) | copy-start | bytes 24580
  7.2 53.5 %all-reduce.2.cloned.1.call-start = ((), (), s32[]{:S(2)}) async-start(), calls=%async_computation.1 | async-start | bytes 1048576 | tf_op jit(solution)/shard_map/psum | solution.py:78
  8.4 6.8 %collective-permute-start = (bf16[4,3,2048]{2,0,1:T(4,128)(2,1)S(1)}, bf16[4,3,2048]{2,0,1:T(4,128)(2,1)S(1)}, u32[]{:S(2)}, u32[]{:S(2)}) collective-permute-start(bf16[4,3,2048]{2,0,1:T(4,128)(2,1)S(1)} %copy.48), channel_id=1, source_target_pairs={{0,4},{4,8},{8,12},{12,16},{16,20},{20,24},{24,28},{1,5},{5,9},{9,... | collective-permute-start | bytes 147464 | tf_op jit(solution)/shard_map/ppermute | solution.py:10
  18.3 5.5 %copy-start.10 = (bf16[2048,512]{1,0:T(8,128)(2,1)S(1)}, bf16[2048,512]{1,0:T(8,128)(2,1)}, u32[]{:S(2)}) copy-start(bf16[2048,512]{1,0:T(8,128)(2,1)} %param.25) | copy-start | bytes 6291460
  22.5 1.3 copy-start.3
  22.5 3.4 copy-start.6
  25.9 103.6 %all-gather.4.cloned.1.call-start = ((), (), s32[]{:S(2)}) async-start(), calls=%async_computation.2 | async-start | bytes 2359296 | tf_op jit(solution)/shard_map/all_gather | solution.py:16
  39.5 22.4 %copy-start.7 = (f32[2048]{0:T(1024)S(1)}, f32[2048]{0:T(1024)}, u32[]{:S(2)}) copy-start(f32[2048]{0:T(1024)} %param.28) | copy-start | bytes 24580
  72.2 106.4 %all-gather.6.cloned.1.call-start = ((), (), s32[]{:S(2)}) async-start(), calls=%async_computation.4 | async-start | bytes 2359296 | tf_op jit(solution)/shard_map/all_gather | solution.py:16
  129.3 257.6 %reduce-scatter.2.cloned.1.call-start = ((), (), s32[]{:S(2)}) async-start(), calls=%async_computation.3 | async-start | bytes 10485760 | tf_op jit(solution)/shard_map/reduce_scatter | solution.py:112
  178.7 1.0 copy-start.5
  179.8 94.5 %copy-start.9 = (f32[2048]{0:T(1024)S(1)}, f32[2048]{0:T(1024)}, u32[]{:S(2)}) copy-start(f32[2048]{0:T(1024)} %param.30) | copy-start | bytes 24580
  274.3 8.1 %copy-start.2 = (f32[4,16,2048]{2,1,0:T(8,128)}, f32[4,16,2048]{2,1,0:T(8,128)S(1)}, u32[]{:S(2)}) copy-start(f32[4,16,2048]{2,1,0:T(8,128)S(1)} %get-tuple-element.115) | copy-start | bytes 1572868
  386.9 2.3 copy-start.4
  389.2 2.1 copy-start.1
Sparse Core Ops, SparseCore 0:
  26.0 34.5 all-reduce.1
  72.4 49.1 all-gather.3
  129.5 49.1 all-gather.5
  308.5 78.3 reduce-scatter.1
where the time goes:
time: 404 us; the launch traced here: 398 us
  waiting for transfers between devices  142 us (35%)
  other arithmetic  128 us (32%)
  local copies, waits for them, and re-layouts  62.6 us (15%)
  matrix products  32.9 us (8%)
  between operations  14.1 us (3%)
  blocking collectives  10.8 us (3%)
  starting transfers between devices  5.26 us (1%)
    reduce_scatter x1, waiting for transfers between devices, body(): lax.psum_scatter(lax.dot_general(out_weight, flat_rows, (((0,), (1,)), ((...  78.5 us
    all_gather x2, waiting for transfers between devices, carried_in(): lax.all_gather(a.astype(kind), axis)  49.1 us
    reduce_sum x48, other arithmetic, advance(): emitted = jnp.sum(read_c[:, :, None] * carried, axis=1)  47.4 us
    mul x32, other arithmetic, advance(): step_dt * value_x  34.7 us
    mul x32, local copies, waits for them, and re-layouts, advance(): factor = jnp.exp(decay_rates[None, :, :] * step_dt[:, None, :])  29.2 us
    dot_general x1, matrix products, body(): lax.dot_general(out_weight, flat_rows, (((0,), (1,)), ((), ())), preferre...  26 us
    add x16, other arithmetic, advance(): factor * carried + (step_dt * value_x)[:, None, :] * gate_b[:, :, None]  15.9 us
    psum x1, waiting for transfers between devices, body(): lax.psum(low_part.astype(jnp.bfloat16), 'tp').astype(jnp.float32)  14.3 us
  transfers between devices with their start and end apart: 5, of which 3 were waited for; matrix products, arithmetic and copies ran while one was open for 17% of the time, Pallas kernels for 0%

commit v1 on v0

v1 whole, which is shorter than its diff:
```python
import functools

import jax
import jax.numpy as jnp
from jax import lax
from jax.experimental import pallas as pl
from jax.experimental.pallas import tpu as pltpu
from jax.sharding import PartitionSpec as P

LANES = 128
SUBLANES = 8
TILE = LANES * SUBLANES
LOG2E = 1.4426950408889634
VMEM_LIMIT = 40 * 2**20


def swapped(x, axis, bit):
    return lax.ppermute(x, axis, [(i, i ^ bit) for i in range(lax.axis_size(axis))])


def bits_of(axis):
    bit, found = 1, []
    while bit < lax.axis_size(axis):
        found.append(bit)
        bit *= 2
    return found


def to_rows(x):
    return x.reshape(*x.shape[:-1], -1, SUBLANES, LANES)


def spread(bc_ref, wide_ref, count):
    tokens = bc_ref.shape[0]
    for n in range(count):
        wide_ref[pl.ds(n * tokens, tokens), :] = jnp.broadcast_to(
            bc_ref[:, n : n + 1], (tokens, LANES)
        )


def scan_tokens(dt_ref, u_ref, wide_ref, rate_ref, first, states, tokens, y_ref, unroll):
    rates = [rate_ref[n] for n in range(states)]

    def group(i, held):
        held = list(held)
        for j in range(unroll):
            t = i * unroll + j
            base = i * (unroll * SUBLANES) + (j // SUBLANES) * SUBLANES * SUBLANES
            rows = pl.ds(base + j % SUBLANES, SUBLANES, stride=SUBLANES)
            dt = dt_ref[rows, :]
            u = u_ref[rows, :]
            y = None
            for n in range(states):
                gate = wide_ref[pl.ds(n * tokens + t, SUBLANES, stride=0), :]
                held[n] = jnp.exp2(rates[n] * dt) * held[n] + u * gate
                if y_ref is not None:
                    read = wide_ref[pl.ds((states + n) * tokens + t, SUBLANES, stride=0), :]
                    part = read * held[n]
                    y = part if y is None else y + part
            if y_ref is not None:
                y_ref[rows, :] = y
        return tuple(held)

    return lax.fori_loop(0, tokens // unroll, group, tuple(first))


def steps_kernel(
    states, normed_ref, weight_ref, bias_ref, act_ref, bc_ref, rate_ref,
    dt_ref, end_ref, elapsed_ref, u_ref, wide_ref,
):
    tokens = normed_ref.shape[0]
    spread(bc_ref, wide_ref, states)
    raw = jnp.dot(normed_ref[...], weight_ref[...], preferred_element_type=jnp.float32)
    raw = raw + bias_ref[...]
    dt = jnp.maximum(raw, 0.0) + jnp.log1p(jnp.exp(-jnp.abs(raw)))
    u = dt * act_ref[...].astype(jnp.float32)
    total = jnp.sum(dt, axis=0, keepdims=True)
    for g in range(SUBLANES):
        elapsed_ref[g : g + 1, :] = total[:, g * LANES : (g + 1) * LANES]
        for i in range(tokens // SUBLANES):
            rows = pl.ds((i * SUBLANES + g) * SUBLANES, SUBLANES)
            part = (slice(i * SUBLANES, (i + 1) * SUBLANES), slice(g * LANES, (g + 1) * LANES))
            dt_ref[rows, :] = dt[part]
            u_ref[rows, :] = u[part]
    zero = [jnp.zeros((SUBLANES, LANES), jnp.float32)] * states
    held = scan_tokens(dt_ref, u_ref, wide_ref, rate_ref, zero, states, tokens, None, 16)
    for n in range(states):
        end_ref[n] = held[n]


def steps_call(normed, weight, bias, act, bc, rates):
    seqs, tokens, rank = normed.shape
    tiles, states = rates.shape[0], rates.shape[1]
    sq = pl.Squeezed()
    rows = tokens * SUBLANES
    return pl.pallas_call(
        functools.partial(steps_kernel, states),
        out_shape=(
            jax.ShapeDtypeStruct((seqs, tiles, rows, LANES), jnp.float32),
            jax.ShapeDtypeStruct((seqs, tiles, states, SUBLANES, LANES), jnp.float32),
            jax.ShapeDtypeStruct((seqs, tiles, SUBLANES, LANES), jnp.float32),
        ),
        grid=(tiles, seqs),
        in_specs=[
            pl.BlockSpec((sq, tokens, rank), lambda c, s: (s, 0, 0)),
            pl.BlockSpec((rank, TILE), lambda c, s: (0, c)),
            pl.BlockSpec((1, TILE), lambda c, s: (0, c)),
            pl.BlockSpec((sq, tokens, TILE), lambda c, s: (s, 0, c)),
            pl.BlockSpec((sq, tokens, bc.shape[2]), lambda c, s: (s, 0, 0)),
            pl.BlockSpec((sq, states, SUBLANES, LANES), lambda c, s: (c, 0, 0, 0)),
        ],
        out_specs=(
            pl.BlockSpec((sq, sq, rows, LANES), lambda c, s: (s, c, 0, 0)),
            pl.BlockSpec((sq, sq, states, SUBLANES, LANES), lambda c, s: (s, c, 0, 0, 0)),
            pl.BlockSpec((sq, sq, SUBLANES, LANES), lambda c, s: (s, c, 0, 0)),
        ),
        scratch_shapes=[
            pltpu.VMEM((rows, LANES), jnp.float32),
            pltpu.VMEM((states * tokens, LANES), jnp.float32),
        ],
        compiler_params=pltpu.CompilerParams(vmem_limit_bytes=VMEM_LIMIT),
        cost_estimate=pl.CostEstimate(
            flops=2 * seqs * tokens * rank * tiles * TILE,
            bytes_accessed=8 * seqs * tokens * tiles * TILE,
            transcendentals=seqs * tokens * tiles * TILE * states,
        ),
    )(normed, weight, bias[None], act, bc, rates)


def scan_kernel(
    states, dt_ref, act_ref, z_ref, bc_ref, rate_ref, enter_ref, skip_ref,
    gated_ref, final_ref, u_ref, y_ref, wide_ref,
):
    tokens = act_ref.shape[0]
    spread(bc_ref, wide_ref, 2 * states)
    tiles = [(i, g) for i in range(tokens // SUBLANES) for g in range(SUBLANES)]

    def place(i, g):
        rows = pl.ds((i * SUBLANES + g) * SUBLANES, SUBLANES)
        return rows, pl.ds(i * SUBLANES, SUBLANES), pl.ds(g * LANES, LANES)

    for i, g in tiles:
        rows, at, lanes = place(i, g)
        u_ref[rows, :] = dt_ref[rows, :] * act_ref[at, lanes].astype(jnp.float32)
    first = [enter_ref[n] for n in range(states)]
    held = scan_tokens(dt_ref, u_ref, wide_ref, rate_ref, first, states, tokens, y_ref, 16)
    for n in range(states):
        for g in range(SUBLANES):
            final_ref[n : n + 1, g * LANES : (g + 1) * LANES] = held[n][g : g + 1, :]
    for i in range(tokens // 16):
        for g in range(SUBLANES):
            lanes = pl.ds(g * LANES, LANES)
            at = pl.ds(i * 16, 16)
            y = jnp.concatenate([y_ref[place(2 * i + k, g)[0], :] for k in range(2)], axis=0)
            y = y + skip_ref[0:1, lanes] * act_ref[at, lanes].astype(jnp.float32)
            z = z_ref[at, lanes].astype(jnp.float32)
            gated_ref[at, lanes] = (y * (z / (1.0 + jnp.exp(-z)))).astype(jnp.bfloat16)


def scan_call(dt, act, z, bc, rates, entering, skip):
    seqs, tiles, rows, _ = dt.shape
    tokens, states = act.shape[1], rates.shape[1]
    sq = pl.Squeezed()
    flat = pl.BlockSpec((sq, tokens, TILE), lambda c, s: (s, 0, c))
    return pl.pallas_call(
        functools.partial(scan_kernel, states),
        out_shape=(
            jax.ShapeDtypeStruct((seqs, tokens, tiles * TILE), jnp.bfloat16),
            jax.ShapeDtypeStruct((seqs, states, tiles * TILE), jnp.float32),
        ),
        grid=(tiles, seqs),
        in_specs=[
            pl.BlockSpec((sq, sq, rows, LANES), lambda c, s: (s, c, 0, 0)),
            flat,
            flat,
            pl.BlockSpec((sq, tokens, bc.shape[2]), lambda c, s: (s, 0, 0)),
            pl.BlockSpec((sq, states, SUBLANES, LANES), lambda c, s: (c, 0, 0, 0)),
            pl.BlockSpec((sq, sq, states, SUBLANES, LANES), lambda c, s: (s, c, 0, 0, 0)),
            pl.BlockSpec((1, TILE), lambda c, s: (0, c)),
        ],
        out_specs=(flat, pl.BlockSpec((sq, states, TILE), lambda c, s: (s, 0, c))),
        scratch_shapes=[
            pltpu.VMEM((rows, LANES), jnp.float32),
            pltpu.VMEM((rows, LANES), jnp.float32),
            pltpu.VMEM((2 * states * tokens, LANES), jnp.float32),
        ],
        compiler_params=pltpu.CompilerParams(vmem_limit_bytes=VMEM_LIMIT),
        cost_estimate=pl.CostEstimate(
            flops=6 * seqs * tokens * tiles * TILE * states,
            bytes_accessed=10 * seqs * tokens * tiles * TILE,
            transcendentals=seqs * tokens * tiles * TILE * states,
        ),
    )(dt, act, z, bc, rates, entering, skip[None])


def out_kernel(me_ref, x_ref, w_ref, o_ref):
    o_ref[...] = jnp.dot(x_ref[...], w_ref[...], preferred_element_type=jnp.float32).astype(
        o_ref.dtype
    )


def out_call(me, x, weight, groups, piece, pieces):
    rows, depth = x.shape
    own = weight.shape[1] // groups
    width = own // pieces
    step = min(width, 512)
    steps = width // step
    sq = pl.Squeezed()
    return pl.pallas_call(
        out_kernel,
        out_shape=jax.ShapeDtypeStruct((groups, rows, width), jnp.bfloat16),
        grid_spec=pltpu.PrefetchScalarGridSpec(
            num_scalar_prefetch=1,
            grid=(groups, steps),
            in_specs=[
                pl.BlockSpec((rows, depth), lambda j, k, me: (0, 0)),
                pl.BlockSpec(
                    (depth, step),
                    lambda j, k, me: (0, ((groups - 1 - j) ^ me[0]) * (own // step) + piece * steps + k),
                ),
            ],
            out_specs=pl.BlockSpec((sq, rows, step), lambda j, k, me: (groups - 1 - j, 0, k)),
        ),
        compiler_params=pltpu.CompilerParams(vmem_limit_bytes=VMEM_LIMIT),
        cost_estimate=pl.CostEstimate(
            flops=2 * rows * depth * width * groups,
            bytes_accessed=2 * depth * width * groups,
            transcendentals=0,
        ),
    )(me, x, weight)


def scattered(parts, axis):
    held = [parts]
    for bit in bits_of(axis):
        cut = [p.reshape(p.shape[0] // 2, 2, *p.shape[1:]) for p in held]
        keep = [p[:, 0] for p in cut]
        gone = functools.reduce(
            jnp.add, [p[:, 1].astype(jnp.float32) for p in cut]
        ).astype(jnp.bfloat16)
        held = keep + [swapped(gone, axis, bit)]
    return functools.reduce(jnp.add, [p[0].astype(jnp.float32) for p in held])


def carried(end, elapsed, rates):
    place = lax.axis_index("seq")
    decayed = lambda time, state: jnp.exp2(rates * time[:, :, None]) * state
    prior_time, prior = jnp.zeros_like(elapsed), jnp.zeros_like(end)
    time, state = elapsed, end
    bits = bits_of("seq")
    for bit in bits:
        high = time.astype(jnp.bfloat16)
        low = (time - high.astype(jnp.float32)).astype(jnp.bfloat16)
        sent = jnp.concatenate(
            [state.astype(jnp.bfloat16), high[:, :, None], low[:, :, None]], axis=2
        )
        came = swapped(sent, "seq", bit).astype(jnp.float32)
        their_state, their_time = came[:, :, :-2], came[:, :, -2] + came[:, :, -1]
        late = (place & bit) != 0
        prior = jnp.where(late, decayed(prior_time, their_state) + prior, prior)
        prior_time = jnp.where(late, prior_time + their_time, prior_time)
        if bit != bits[-1]:
            state = jnp.where(
                late,
                decayed(time, their_state) + state,
                decayed(their_time, state) + their_state,
            )
            time = time + their_time
    return prior_time, prior


def summed(part, axis):
    for bit in bits_of(axis):
        sent = part if bit == 1 else part.astype(jnp.bfloat16)
        part = part + swapped(sent, axis, bit).astype(jnp.float32)
    return part


def body(
    inner_x, inner_z, conv_tail, conv_weight, conv_bias, xproj_dt, xproj_bc, dt_weight, dt_bias,
    decay_log, skip_gain, out_weight, residual, init_state,
):
    seqs, length, channels = inner_x.shape
    kernel = conv_weight.shape[0]
    states = init_state.shape[1]
    rank = xproj_dt.shape[1]
    groups = lax.axis_size("tp")
    chunks = 2
    pieces = 2
    per = seqs // chunks
    me = lax.axis_index("tp").astype(jnp.int32)[None]

    rim = inner_x[:, length - (kernel - 1) :, :]
    blocks = lax.axis_size("seq")
    arrived = lax.ppermute(rim, "seq", [(i, i + 1) for i in range(blocks - 1)])
    earlier = jnp.where(lax.axis_index("seq") == 0, conv_tail, arrived)
    xproj = jnp.concatenate([xproj_dt, xproj_bc], axis=1)
    rates = jnp.swapaxes(to_rows(-jnp.exp(decay_log) * LOG2E), 0, 1)
    start = jnp.swapaxes(to_rows(init_state), 1, 2)

    acts, gates, times, ends, elapsed = [], [], [], [], []
    for c in range(chunks):
        mine = slice(c * per, (c + 1) * per)
        joined = jnp.concatenate([earlier[mine], inner_x[mine]], axis=1).astype(jnp.float32)
        mixed = conv_bias + conv_weight[0] * joined[:, 0:length, :]
        for offset in range(1, kernel):
            mixed = mixed + conv_weight[offset] * joined[:, offset : offset + length, :]
        act = jax.nn.silu(mixed).astype(jnp.bfloat16)
        part = jnp.dot(act, xproj, preferred_element_type=jnp.float32)
        both = summed(part, "tp")
        low, bc = both[..., :rank], both[..., rank:]
        normed = (
            low * lax.rsqrt(jnp.mean(low * low, axis=-1, keepdims=True) + 1e-06)
        ).astype(jnp.bfloat16)
        dt, end, time = steps_call(normed, dt_weight, dt_bias, act, bc, rates)
        acts.append(act)
        gates.append(bc)
        times.append(dt)
        ends.append(end)
        elapsed.append(time)
    hidden, finals = [], []
    for c in range(chunks):
        mine = slice(c * per, (c + 1) * per)
        prior_time, prior = carried(ends[c], elapsed[c], rates)
        entering = jnp.exp2(rates * prior_time[:, :, None]) * start[mine] + prior
        gated, final = scan_call(
            times[c], acts[c], inner_z[mine], gates[c], rates, entering, skip_gain
        )
        finals.append(final)
        flat = gated.reshape(-1, channels)
        outs = []
        for p in range(pieces):
            own = scattered(out_call(me, flat, out_weight, groups, p, pieces), "tp")
            width = own.shape[-1]
            base = residual[mine, :, p * width : (p + 1) * width].astype(jnp.float32)
            outs.append((base + own.reshape(base.shape)).astype(jnp.bfloat16))
        hidden.append(jnp.concatenate(outs, axis=-1))
    return jnp.concatenate(hidden, axis=0), jnp.concatenate(finals, axis=0)[None]


def solution(mesh):
    return jax.shard_map(
        body,
        mesh=mesh,
        in_specs=(
            P(None, "seq", "tp"),
            P(None, "seq", "tp"),
            P(None, None, "tp"),
            P(None, "tp"),
            P("tp"),
            P("tp", None),
            P("tp", None),
            P(None, "tp"),
            P("tp"),
            P(None, "tp"),
            P("tp"),
            P("tp", None),
            P(None, "seq", "tp"),
            P(None, None, "tp"),
        ),
        out_specs=(P(None, "seq", "tp"), P("seq", None, None, "tp")),
        check_vma=False,
    )
```

time: 404 us -> 214 us (0.53); the launches traced: 398 us -> 213 us
  other arithmetic: 128 us -> 15.3 us
  Pallas kernels: 0 us -> 83.4 us
  waiting for transfers between devices: 142 us -> 68.7 us
  local copies, waits for them, and re-layouts: 62.6 us -> 19 us
  matrix products: 32.9 us -> 3.2 us
  starting transfers between devices: 5.26 us -> 22.5 us
  between operations: 14.1 us -> 1.32 us
  blocking collectives: 10.8 us -> 0 us
    pallas_call x0 -> x8, Pallas kernels: none -> 83.4 us  [the longest x4 42.2 us: out_call(): pl.pallas_call(out_kernel, out_shape=jax.ShapeDtypeStruct((groups, rows,...]
    reduce_scatter x1 -> x0, waiting for transfers between devices: 78.5 us -> none  [body(): lax.psum_scatter(lax.dot_general(out_weight, flat_rows, (((0,), (1,)), ((...]
    ppermute x1 -> x19, waiting for transfers between devices: 0.01 us -> 68.7 us  [the longest x18 68.7 us: swapped(): lax.ppermute(x, axis, [(i, i ^ bit) for i in range(lax.axis_size(axis))])]
    reduce_sum x50 -> x2, other arithmetic: 51.3 us -> 0.23 us  [body(): jnp.mean(low * low, axis=-1, keepdims=True) + 1e-06]
    all_gather x2 -> x0, waiting for transfers between devices: 49.1 us -> none  [carried_in(): lax.all_gather(a.astype(kind), axis)]
    mul x32 -> x4, other arithmetic: 34.7 us -> 0.04 us  [the longest x2 0.02 us: body(): entering = jnp.exp2(rates * prior_time[:, :, None]) * start[mine] + prior]
    mul x64 -> x0, local copies, waits for them, and re-layouts: 30.1 us -> none  [the longest x32 29.2 us: advance(): factor = jnp.exp(decay_rates[None, :, :] * step_dt[:, None, :])]
    dot_general x4 -> x2, matrix products: 32.9 us -> 3.2 us  [body(): part = jnp.dot(act, xproj, preferred_element_type=jnp.float32)]
  transfers between devices with their start and end apart: 5 -> 19, of which waited for: 3 -> 11; matrix products, arithmetic and copies ran while one was open for 17% -> 12% of each run, Pallas kernels for 0% -> 19%
where the time goes in v1:
time: 214 us; the launch traced here: 213 us
  Pallas kernels  83.4 us (39%)
  waiting for transfers between devices  68.7 us (32%)
  starting transfers between devices  22.5 us (11%)
  local copies, waits for them, and re-layouts  19 us (9%)
  other arithmetic  15.3 us (7%)
  matrix products  3.2 us (1%)
    ppermute x18, waiting for transfers between devices, swapped(): lax.ppermute(x, axis, [(i, i ^ bit) for i in range(lax.axis_size(axis))])  68.7 us
    pallas_call x4, Pallas kernels, out_call(): pl.pallas_call(out_kernel, out_shape=jax.ShapeDtypeStruct((groups, rows,...  42.2 us
    pallas_call x2, Pallas kernels, scan_call(): pl.pallas_call(functools.partial(scan_kernel, states), out_shape=(jax.Sha...  24.4 us
    ppermute x18, starting transfers between devices, swapped(): lax.ppermute(x, axis, [(i, i ^ bit) for i in range(lax.axis_size(axis))])  17.5 us
    pallas_call x2, Pallas kernels, steps_call(): pl.pallas_call(functools.partial(steps_kernel, states), out_shape=(jax.Sh...  16.9 us
    ppermute x1, starting transfers between devices, body(): arrived = lax.ppermute(rim, 'seq', [(i, i + 1) for i in range(blocks - 1)])  5.01 us
    unnamed x33, local copies, waits for them, and re-layouts  4.99 us
  transfers between devices with their start and end apart: 19, of which 11 were waited for; matrix products, arithmetic and copies ran while one was open for 12% of the time, Pallas kernels for 19%

profile of v1, /device:TPU:0, one launch (start us, length us, event | category | flops | bytes accessed | tf_op | source)
XLA Modules:
  0.0 213.4 jit_solution(1702776111228618355)
XLA Ops:
  0.6 0.9 slice.219
  1.6 5.0 %collective-permute-start = (bf16[4,3,2048]{2,1,0:T(4,128)(2,1)S(1)}, bf16[4,3,2048]{2,1,0:T(4,128)(2,1)S(1)}, u32[]{:S(2)}, u32[]{:S(2)}) collective-permute-start(bf16[4,3,2048]{2,1,0:T(4,128)(2,1)S(1)} %slice.219), channel_id=1, source_target_pairs={{0,4},{4,8},{8,12},{12,16},{16,20},{20,24},{24,28},{1,5},{5,9},{9,... | collective-permute-start | bytes 147464 | tf_op jit(solution)/shard_map/ppermute | solution.py:295
  6.6 1.7 fusion.47
  8.5 4.0 %copy.86 = bf16[2048,512]{0,1:T(8,128)(2,1)} copy(bf16[2048,512]{1,0:T(8,128)(2,1)} %param.19) | data formatting | bytes 4194304 | tf_op args[5]
  12.6 0.8 copy.166
  13.6 0.7 maximum_convert_fusion
  14.3 2.7 %multiply_convert_fusion.1 = (bf16[2,128,2048]{2,1,0:T(8,128)(2,1)S(1)}, bf16[2,128,2048]{2,1,0:T(8,128)(2,1)S(1)}) fusion(f32[2,131,2048]{2,1,0:T(8,128)S(1)} %get-tuple-element.86, f32[2048]{0:T(1024)S(1)} %bitcast.229, f32[2048]{0:T(1024)S(1)} %bitcast.230, f32[2048]{0:T(1024)S(1)} %bitcast.228, f32[2048]{0:T(1024)S(1)} %bitcast.227, ...), kind=kLoop, calls=%fused_computation.19 | loop fusion | flops 13631488 | bytes 18915328 | tf_op jit(solution)/shard_map/convert_element_type | solution.py:308
  17.0 1.6 fusion.8
  18.6 1.6 fusion.9
  20.2 0.5 collective-permute-start.1
  20.7 1.1 fusion.46
  21.8 2.1 copy.99
  24.0 2.1 copy.87
  26.1 2.1 copy.100
  28.2 2.3 %fusion.45 = (bf16[2,128,544]{2,1,0:T(8,128)(2,1)}, f32[2,128,544]{2,1,0:T(8,128)}) fusion(f32[2,128,544]{2,1,0:T(8,128)} %copy.99, f32[2,128,544]{2,1,0:T(8,128)} %copy.100), kind=kLoop, calls=%fused_computation.142 | loop fusion | flops 278528 | bytes 1949696 | tf_op jit(solution)/shard_map/convert_element_type | solution.py:274
  30.5 1.5 collective-permute-start.11
  32.1 2.1 copy.88
  34.2 1.4 fusion.43
  35.6 0.6 collective-permute-start.2
  36.2 5.2 %collective-permute-done.11 = bf16[2,128,544]{2,1,0:T(8,128)(2,1)} collective-permute-done((bf16[2,128,544]{2,1,0:T(8,128)(2,1)}, bf16[2,128,544]{2,1,0:T(8,128)(2,1)}, u32[]{:S(2)}, u32[]{:S(2)}) %collective-permute-start.11) | collective-permute-done | bytes 278560 | tf_op jit(solution)/shard_map/ppermute | solution.py:18
  41.4 1.0 convert_add_fusion.8
  42.6 4.8 %collective-permute-done.2 = bf16[2,128,544]{2,1,0:T(8,128)(2,1)S(1)} collective-permute-done((bf16[2,128,544]{2,1,0:T(8,128)(2,1)S(1)}, bf16[2,128,544]{2,1,0:T(8,128)(2,1)S(1)}, u32[]{:S(2)}, u32[]{:S(2)}) %collective-permute-start.2) | collective-permute-done | bytes 278560 | tf_op jit(solution)/shard_map/ppermute | solution.py:18
  47.7 8.4 %shard_map.153 = (f32[2,2,1024,128]{3,2,1,0:T(8,128)S(1)}, f32[2,2,16,8,128]{4,3,2,1,0:T(8,128)S(1)}, f32[2,2,8,128]{3,2,1,0:T(8,128)S(1)}) custom-call(bf16[2,128,512]{2,1,0:T(8,128)(2,1)S(1)} %multiply_convert_fusion.2.normed_ref, bf16[512,2048]{1,0:T(8,128)(2,1)S(1)} %copy-done.1, f32[1,2048]{1,0:T(1,128)S(1)} %bitcast.195, ...), custom_call_target="tpu_custom_call" | custom-call | flops 536870912 | bytes 4194304 | tf_op jit(solution)/shard_map/pallas_call | solution.py:96
  56.2 1.6 collective-permute-start.12
  58.0 8.4 %shard_map.149 = (f32[2,2,1024,128]{3,2,1,0:T(8,128)S(1)}, f32[2,2,16,8,128]{4,3,2,1,0:T(8,128)S(1)}, f32[2,2,8,128]{3,2,1,0:T(8,128)S(1)}) custom-call(bf16[2,128,512]{2,1,0:T(8,128)(2,1)S(1)} %multiply_convert_fusion.3.normed_ref, bf16[512,2048]{1,0:T(8,128)(2,1)S(1)} %copy-done.1, f32[1,2048]{1,0:T(1,128)S(1)} %bitcast.196, ...), custom_call_target="tpu_custom_call" | custom-call | flops 536870912 | bytes 4194304 | tf_op jit(solution)/shard_map/pallas_call | solution.py:96
  66.5 0.5 collective-permute-start.3
  67.0 4.6 %collective-permute-done.3 = bf16[2,2,18,8,128]{4,3,1,0,2:T(8,128)(2,1)S(1)} collective-permute-done((bf16[2,2,18,8,128]{4,3,1,0,2:T(8,128)(2,1)S(1)}, bf16[2,2,18,8,128]{4,3,1,0,2:T(8,128)(2,1)S(1)}, u32[]{:S(2)}, u32[]{:S(2)}) %collective-permute-start.3) | collective-permute-done | bytes 147488 | tf_op jit(solution)/shard_map/ppermute | solution.py:18
  71.9 1.6 collective-permute-start.4
  73.6 3.9 %collective-permute-done.4 = bf16[2,2,18,8,128]{4,3,1,0,2:T(8,128)(2,1)S(1)} collective-permute-done((bf16[2,2,18,8,128]{4,3,1,0,2:T(8,128)(2,1)S(1)}, bf16[2,2,18,8,128]{4,3,1,0,2:T(8,128)(2,1)S(1)}, u32[]{:S(2)}, u32[]{:S(2)}) %collective-permute-start.4) | collective-permute-done | bytes 147488 | tf_op jit(solution)/shard_map/ppermute | solution.py:18
  77.5 0.4 select_convert_fusion.1
  77.9 1.7 collective-permute-start.13
  79.6 1.1 collective-permute-start.5
  80.7 3.9 %collective-permute-done.13 = bf16[2,2,18,8,128]{4,3,1,0,2:T(8,128)(2,1)S(1)} collective-permute-done((bf16[2,2,18,8,128]{4,3,1,0,2:T(8,128)(2,1)S(1)}, bf16[2,2,18,8,128]{4,3,1,0,2:T(8,128)(2,1)S(1)}, u32[]{:S(2)}, u32[]{:S(2)}) %collective-permute-start.13) | collective-permute-done | bytes 147488 | tf_op jit(solution)/shard_map/ppermute | solution.py:18
  84.6 0.3 multiply_add_fusion
  85.0 2.7 %collective-permute-start.14 = (bf16[2,2,18,8,128]{4,3,1,0,2:T(8,128)(2,1)S(1)}, bf16[2,2,18,8,128]{4,3,1,0,2:T(8,128)(2,1)S(1)}, u32[]{:S(2)}, u32[]{:S(2)}) collective-permute-start(bf16[2,2,18,8,128]{4,3,1,0,2:T(8,128)(2,1)S(1)} %pad_maximum_fusion.5), channel_id=1, source_target_pairs={{0,16},{4,20},{8,24},{12,28},{16,0},{20,4},{24,8},{28,12},{1,17},{... | collective-permute-start | bytes 442376 | tf_op jit(solution)/shard_map/ppermute | solution.py:18
  87.7 1.1 collective-permute-done.5
  88.9 3.8 %collective-permute-done.14 = bf16[2,2,18,8,128]{4,3,1,0,2:T(8,128)(2,1)S(1)} collective-permute-done((bf16[2,2,18,8,128]{4,3,1,0,2:T(8,128)(2,1)S(1)}, bf16[2,2,18,8,128]{4,3,1,0,2:T(8,128)(2,1)S(1)}, u32[]{:S(2)}, u32[]{:S(2)}) %collective-permute-start.14) | collective-permute-done | bytes 147488 | tf_op jit(solution)/shard_map/ppermute | solution.py:18
  92.8 0.3 fusion.22
  93.1 0.8 copy-done
  93.9 12.2 %shard_map.154 = (bf16[2,128,2048]{2,1,0:T(8,128)(2,1)S(1)}, f32[2,16,2048]{2,1,0:T(8,128)S(1)}) custom-call(f32[2,2,1024,128]{3,2,1,0:T(8,128)S(1)} %get-tuple-element.16.dt_ref, bf16[2,128,2048]{2,1,0:T(8,128)(2,1)S(1)} %get-tuple-element.77.act_ref, bf16[2,128,2048]{2,1,0:T(8,128)(2,1)S(1)} %copy-done, f32[2,128,32]{2,1,0:T(8,128)S(1)} %slice.323.bc_ref, ...), custom_call_target="tpu_custom_call" | custom-call | flops 50331648 | bytes 5242880 | tf_op jit(solution)/shard_map/pallas_call | solution.py:165
  106.1 10.5 %shard_map.155 = bf16[4,256,1024]{2,1,0:T(8,128)(2,1)S(1)} custom-call(s32[1]{0:T(128)} %bitcast.me_ref, bf16[256,2048]{1,0:T(8,128)(2,1)S(1)} %bitcast.189, bf16[2048,8192]{1,0:T(8,128)(2,1)} %w_ref.7), custom_call_target="tpu_custom_call" | custom-call | flops 4294967296 | bytes 16777216 | tf_op jit(solution)/shard_map/pallas_call | solution.py:209
  116.6 10.7 %shard_map.156 = bf16[4,256,1024]{2,1,0:T(8,128)(2,1)S(1)} custom-call(s32[1]{0:T(128)} %bitcast.me_ref, bf16[256,2048]{1,0:T(8,128)(2,1)S(1)} %bitcast.190, bf16[2048,8192]{1,0:T(8,128)(2,1)} %w_ref.7), custom_call_target="tpu_custom_call" | custom-call | flops 4294967296 | bytes 16777216 | tf_op jit(solution)/shard_map/pallas_call | solution.py:209
  127.6 0.2 slice_bitcast_fusion.1
  127.8 0.6 collective-permute-start.17
  128.3 12.2 %shard_map.150 = (bf16[2,128,2048]{2,1,0:T(8,128)(2,1)S(1)}, f32[2,16,2048]{2,1,0:T(8,128)S(1)}) custom-call(f32[2,2,1024,128]{3,2,1,0:T(8,128)S(1)} %get-tuple-element.12.dt_ref, bf16[2,128,2048]{2,1,0:T(8,128)(2,1)S(1)} %get-tuple-element.76.act_ref, bf16[2,128,2048]{2,1,0:T(8,128)(2,1)S(1)} %get-tuple-element.56.z_ref, f32[2,128,32]{2,1,0:T(8,128)S(1)} %slice.294.bc_ref, ...), custom_call_target="tpu_custom_call" | custom-call | flops 50331648 | bytes 5242880 | tf_op jit(solution)/shard_map/pallas_call | solution.py:165
  140.5 10.5 %shard_map.152 = bf16[4,256,1024]{2,1,0:T(8,128)(2,1)S(1)} custom-call(s32[1]{0:T(128)} %bitcast.me_ref, bf16[256,2048]{1,0:T(8,128)(2,1)S(1)} %bitcast.187, bf16[2048,8192]{1,0:T(8,128)(2,1)} %w_ref.7), custom_call_target="tpu_custom_call" | custom-call | flops 4294967296 | bytes 16777216 | tf_op jit(solution)/shard_map/pallas_call | solution.py:209
  151.3 10.5 %shard_map.151 = bf16[4,256,1024]{2,1,0:T(8,128)(2,1)S(1)} custom-call(s32[1]{0:T(128)} %bitcast.me_ref, bf16[256,2048]{1,0:T(8,128)(2,1)S(1)} %bitcast.188, bf16[2048,8192]{1,0:T(8,128)(2,1)} %w_ref.7), custom_call_target="tpu_custom_call" | custom-call | flops 4294967296 | bytes 16777216 | tf_op jit(solution)/shard_map/pallas_call | solution.py:209
  161.8 0.3 slice_bitcast_fusion.7
  162.1 0.5 collective-permute-start.6
  162.6 0.4 fusion.20
  163.0 1.6 collective-permute-start.16
  164.6 0.4 fusion.21
  164.9 0.6 collective-permute-start.18
  165.5 0.4 fusion.19
  165.9 1.6 collective-permute-start.9
  167.5 0.4 fusion.18
  167.8 0.6 collective-permute-start.7
  168.4 0.8 maximum_bitcast_fusion.3
  169.3 8.6 %collective-permute-done.16 = bf16[1,256,1024]{2,1,0:T(8,128)(2,1)S(1)} collective-permute-done((bf16[1,256,1024]{2,1,0:T(8,128)(2,1)S(1)}, bf16[1,256,1024]{2,1,0:T(8,128)(2,1)S(1)}, u32[]{:S(2)}, u32[]{:S(2)}) %collective-permute-start.16) | collective-permute-done | bytes 524320 | tf_op jit(solution)/shard_map/ppermute | solution.py:18
  177.8 11.2 %collective-permute-done.18 = bf16[1,256,1024]{2,1,0:T(8,128)(2,1)S(1)} collective-permute-done((bf16[1,256,1024]{2,1,0:T(8,128)(2,1)S(1)}, bf16[1,256,1024]{2,1,0:T(8,128)(2,1)S(1)}, u32[]{:S(2)}, u32[]{:S(2)}) %collective-permute-start.18) | collective-permute-done | bytes 524320 | tf_op jit(solution)/shard_map/ppermute | solution.py:18
  189.1 11.2 %collective-permute-done.9 = bf16[1,256,1024]{2,1,0:T(8,128)(2,1)S(1)} collective-permute-done((bf16[1,256,1024]{2,1,0:T(8,128)(2,1)S(1)}, bf16[1,256,1024]{2,1,0:T(8,128)(2,1)S(1)}, u32[]{:S(2)}, u32[]{:S(2)}) %collective-permute-start.9) | collective-permute-done | bytes 524320 | tf_op jit(solution)/shard_map/ppermute | solution.py:18
  200.3 10.3 %collective-permute-done.7 = bf16[1,256,1024]{2,1,0:T(8,128)(2,1)S(1)} collective-permute-done((bf16[1,256,1024]{2,1,0:T(8,128)(2,1)S(1)}, bf16[1,256,1024]{2,1,0:T(8,128)(2,1)S(1)}, u32[]{:S(2)}, u32[]{:S(2)}) %collective-permute-start.7) | collective-permute-done | bytes 524320 | tf_op jit(solution)/shard_map/ppermute | solution.py:18
  210.6 1.2 fusion.17
  211.9 1.5 maximum_maximum_fusion
  (87 shorter events, 2.0 us)
Async XLA Ops:
  1.6 6.8 %copy-start.12 = (f32[4,2048]{1,0:T(4,128)S(1)}, f32[4,2048]{1,0:T(4,128)}, u32[]{:S(2)}) copy-start(f32[4,2048]{1,0:T(4,128)} %param.17) | copy-start | bytes 98308
  1.6 6.8 %copy-start.10 = (f32[16,2048]{1,0:T(8,128)S(1)}, f32[16,2048]{1,0:T(8,128)}, u32[]{:S(2)}) copy-start(f32[16,2048]{1,0:T(8,128)} %param.23) | copy-start | bytes 393220
  1.6 11.9 %collective-permute-start = (bf16[4,3,2048]{2,1,0:T(4,128)(2,1)S(1)}, bf16[4,3,2048]{2,1,0:T(4,128)(2,1)S(1)}, u32[]{:S(2)}, u32[]{:S(2)}) collective-permute-start(bf16[4,3,2048]{2,1,0:T(4,128)(2,1)S(1)} %slice.219), channel_id=1, source_target_pairs={{0,4},{4,8},{8,12},{12,16},{16,20},{20,24},{24,28},{1,5},{5,9},{9,... | collective-permute-start | bytes 147464 | tf_op jit(solution)/shard_map/ppermute | solution.py:295
  8.4 4.0 %copy-start.9 = (f32[4,16,2048]{2,1,0:T(8,128)S(1)}, f32[4,16,2048]{2,1,0:T(8,128)}, u32[]{:S(2)}) copy-start(f32[4,16,2048]{2,1,0:T(8,128)} %param.27) | copy-start | bytes 1572868
  12.4 1.0 copy-start.11
  13.6 0.7 copy-start.13
  14.3 2.7 %copy-start.8 = (bf16[2048,512]{0,1:T(8,128)(2,1)S(1)}, bf16[2048,512]{0,1:T(8,128)(2,1)}, u32[]{:S(2)}) copy-start(bf16[2048,512]{0,1:T(8,128)(2,1)} %copy.86) | copy-start | bytes 6291460
  14.3 2.7 %copy-start.14 = (bf16[2048,32]{0,1:T(8,128)(2,1)S(1)}, bf16[2048,32]{0,1:T(8,128)(2,1)}, u32[]{:S(2)}) copy-start(bf16[2048,32]{0,1:T(8,128)(2,1)} %param.20) | copy-start | bytes 393220
  18.6 7.5 %collective-permute-start.10 = (f32[2,128,544]{1,2,0:T(8,128)}, f32[2,128,544]{1,2,0:T(8,128)}, u32[]{:S(2)}, u32[]{:S(2)}) collective-permute-start(f32[2,128,544]{1,2,0:T(8,128)} %fusion.8), channel_id=1, source_target_pairs={{0,1},{1,0},{2,3},{3,2},{4,5},{5,4},{6,7},{7,6},{8,9},{9,8},{10,11... | collective-permute-start | bytes 1671176 | tf_op jit(solution)/shard_map/ppermute | solution.py:18
  18.6 2.1 copy-start.7
  20.2 11.8 %collective-permute-start.1 = (f32[2,128,544]{1,2,0:T(8,128)}, f32[2,128,544]{1,2,0:T(8,128)}, u32[]{:S(2)}, u32[]{:S(2)}) collective-permute-start(f32[2,128,544]{1,2,0:T(8,128)} %fusion.9), channel_id=1, source_target_pairs={{0,1},{1,0},{2,3},{3,2},{4,5},{5,4},{6,7},{7,6},{8,9},{9,8},{10,11... | collective-permute-start | bytes 1671176 | tf_op jit(solution)/shard_map/ppermute | solution.py:18
  30.5 10.9 %collective-permute-start.11 = (bf16[2,128,544]{2,1,0:T(8,128)(2,1)}, bf16[2,128,544]{2,1,0:T(8,128)(2,1)}, u32[]{:S(2)}, u32[]{:S(2)}) collective-permute-start(bf16[2,128,544]{2,1,0:T(8,128)(2,1)} %get-tuple-element.42), channel_id=1, source_target_pairs={{0,2},{1,3},{2,0},{3,1},{4,6},{5,7},{6,4},{7,5},{8,10},{9,11},{10,... | collective-permute-start | bytes 835592 | tf_op jit(solution)/shard_map/ppermute | solution.py:18
  34.2 7.3 %copy-start.4 = (f32[2,128,544]{2,1,0:T(8,128)S(1)}, f32[2,128,544]{2,1,0:T(8,128)}, u32[]{:S(2)}) copy-start(f32[2,128,544]{2,1,0:T(8,128)} %get-tuple-element.43) | copy-start | bytes 1671172
  35.6 11.8 %collective-permute-start.2 = (bf16[2,128,544]{2,1,0:T(8,128)(2,1)S(1)}, bf16[2,128,544]{2,1,0:T(8,128)(2,1)S(1)}, u32[]{:S(2)}, u32[]{:S(2)}) collective-permute-start(bf16[2,128,544]{2,1,0:T(8,128)(2,1)S(1)} %get-tuple-element.30), channel_id=1, source_target_pairs={{0,2},{1,3},{2,0},{3,1},{4,6},{5,7},{6,4},{7,5},{8,10},{9,11},{10,... | collective-permute-start | bytes 835592 | tf_op jit(solution)/shard_map/ppermute | solution.py:18
  42.5 5.2 %copy-start.1 = (bf16[512,2048]{1,0:T(8,128)(2,1)S(1)}, bf16[512,2048]{1,0:T(8,128)(2,1)}, u32[]{:S(2)}) copy-start(bf16[512,2048]{1,0:T(8,128)(2,1)} %weight_ref.3) | copy-start | bytes 6291460
  42.5 5.2 %copy-start.2 = (f32[2048]{0:T(1024)S(1)}, f32[2048]{0:T(1024)}, u32[]{:S(2)}) copy-start(f32[2048]{0:T(1024)} %param.22) | copy-start | bytes 24580
  56.2 10.8 %collective-permute-start.12 = (bf16[2,2,18,8,128]{4,3,1,0,2:T(8,128)(2,1)S(1)}, bf16[2,2,18,8,128]{4,3,1,0,2:T(8,128)(2,1)S(1)}, u32[]{:S(2)}, u32[]{:S(2)}) collective-permute-start(bf16[2,2,18,8,128]{4,3,1,0,2:T(8,128)(2,1)S(1)} %pad_maximum_fusion.3), channel_id=1, source_target_pairs={{0,4},{4,0},{8,12},{12,8},{16,20},{20,16},{24,28},{28,24},{1,5},{5... | collective-permute-start | bytes 442376 | tf_op jit(solution)/shard_map/ppermute | solution.py:18
  66.5 5.2 %collective-permute-start.3 = (bf16[2,2,18,8,128]{4,3,1,0,2:T(8,128)(2,1)S(1)}, bf16[2,2,18,8,128]{4,3,1,0,2:T(8,128)(2,1)S(1)}, u32[]{:S(2)}, u32[]{:S(2)}) collective-permute-start(bf16[2,2,18,8,128]{4,3,1,0,2:T(8,128)(2,1)S(1)} %pad_maximum_fusion), channel_id=1, source_target_pairs={{0,4},{4,0},{8,12},{12,8},{16,20},{20,16},{24,28},{28,24},{1,5},{5... | collective-permute-start | bytes 442376 | tf_op jit(solution)/shard_map/ppermute | solution.py:18
  71.9 5.5 %collective-permute-start.4 = (bf16[2,2,18,8,128]{4,3,1,0,2:T(8,128)(2,1)S(1)}, bf16[2,2,18,8,128]{4,3,1,0,2:T(8,128)(2,1)S(1)}, u32[]{:S(2)}, u32[]{:S(2)}) collective-permute-start(bf16[2,2,18,8,128]{4,3,1,0,2:T(8,128)(2,1)S(1)} %pad_maximum_fusion.1), channel_id=1, source_target_pairs={{0,8},{4,12},{8,0},{12,4},{16,24},{20,28},{24,16},{28,20},{1,9},{5... | collective-permute-start | bytes 442376 | tf_op jit(solution)/shard_map/ppermute | solution.py:18
  77.9 14.9 %copy-start.6 = (f32[4,16,2,8,128]{4,3,2,0,1:T(8,128)S(1)}, f32[4,16,2,8,128]{4,3,2,0,1:T(8,128)}, u32[]{:S(2)}) copy-start(f32[4,16,2,8,128]{4,3,2,0,1:T(8,128)} %copy.166) | copy-start | bytes 1572868
  77.9 6.7 %collective-permute-start.13 = (bf16[2,2,18,8,128]{4,3,1,0,2:T(8,128)(2,1)S(1)}, bf16[2,2,18,8,128]{4,3,1,0,2:T(8,128)(2,1)S(1)}, u32[]{:S(2)}, u32[]{:S(2)}) collective-permute-start(bf16[2,2,18,8,128]{4,3,1,0,2:T(8,128)(2,1)S(1)} %pad_maximum_fusion.4), channel_id=1, source_target_pairs={{0,8},{4,12},{8,0},{12,4},{16,24},{20,28},{24,16},{28,20},{1,9},{5... | collective-permute-start | bytes 442376 | tf_op jit(solution)/shard_map/ppermute | solution.py:18
  79.6 9.3 %collective-permute-start.5 = (bf16[2,2,18,8,128]{4,3,1,0,2:T(8,128)(2,1)S(1)}, bf16[2,2,18,8,128]{4,3,1,0,2:T(8,128)(2,1)S(1)}, u32[]{:S(2)}, u32[]{:S(2)}) collective-permute-start(bf16[2,2,18,8,128]{4,3,1,0,2:T(8,128)(2,1)S(1)} %pad_maximum_fusion.2), channel_id=1, source_target_pairs={{0,16},{4,20},{8,24},{12,28},{16,0},{20,4},{24,8},{28,12},{1,17},{... | collective-permute-start | bytes 442376 | tf_op jit(solution)/shard_map/ppermute | solution.py:18
  85.0 7.7 %collective-permute-start.14 = (bf16[2,2,18,8,128]{4,3,1,0,2:T(8,128)(2,1)S(1)}, bf16[2,2,18,8,128]{4,3,1,0,2:T(8,128)(2,1)S(1)}, u32[]{:S(2)}, u32[]{:S(2)}) collective-permute-start(bf16[2,2,18,8,128]{4,3,1,0,2:T(8,128)(2,1)S(1)} %pad_maximum_fusion.5), channel_id=1, source_target_pairs={{0,16},{4,20},{8,24},{12,28},{16,0},{20,4},{24,8},{28,12},{1,17},{... | collective-permute-start | bytes 442376 | tf_op jit(solution)/shard_map/ppermute | solution.py:18
  92.7 1.2 copy-start
  92.7 1.2 copy-start.3
  127.5 35.1 %collective-permute-start.15 = (bf16[2,256,1024]{2,1,0:T(8,128)(2,1)S(1)}, bf16[2,256,1024]{2,1,0:T(8,128)(2,1)S(1)}, u32[]{:S(2)}, u32[]{:S(2)}) collective-permute-start(bf16[2,256,1024]{2,1,0:T(8,128)(2,1)S(1)} %get-tuple-element.63), channel_id=1, source_target_pairs={{0,1},{1,0},{2,3},{3,2},{4,5},{5,4},{6,7},{7,6},{8,9},{9,8},{10,11... | collective-permute-start | bytes 3145736 | tf_op jit(solution)/shard_map/ppermute | solution.py:18
  127.8 36.8 %collective-permute-start.17 = (bf16[2,256,1024]{2,1,0:T(8,128)(2,1)S(1)}, bf16[2,256,1024]{2,1,0:T(8,128)(2,1)S(1)}, u32[]{:S(2)}, u32[]{:S(2)}) collective-permute-start(bf16[2,256,1024]{2,1,0:T(8,128)(2,1)S(1)} %get-tuple-element.67), channel_id=1, source_target_pairs={{0,1},{1,0},{2,3},{3,2},{4,5},{5,4},{6,7},{7,6},{8,9},{9,8},{10,11... | collective-permute-start | bytes 3145736 | tf_op jit(solution)/shard_map/ppermute | solution.py:18
  151.2 14.3 %collective-permute-start.8 = (bf16[2,256,1024]{2,1,0:T(8,128)(2,1)S(1)}, bf16[2,256,1024]{2,1,0:T(8,128)(2,1)S(1)}, u32[]{:S(2)}, u32[]{:S(2)}) collective-permute-start(bf16[2,256,1024]{2,1,0:T(8,128)(2,1)S(1)} %get-tuple-element.55), channel_id=1, source_target_pairs={{0,1},{1,0},{2,3},{3,2},{4,5},{5,4},{6,7},{7,6},{8,9},{9,8},{10,11... | collective-permute-start | bytes 3145736 | tf_op jit(solution)/shard_map/ppermute | solution.py:18
  162.1 5.4 %collective-permute-start.6 = (bf16[2,256,1024]{2,1,0:T(8,128)(2,1)S(1)}, bf16[2,256,1024]{2,1,0:T(8,128)(2,1)S(1)}, u32[]{:S(2)}, u32[]{:S(2)}) collective-permute-start(bf16[2,256,1024]{2,1,0:T(8,128)(2,1)S(1)} %get-tuple-element.51), channel_id=1, source_target_pairs={{0,1},{1,0},{2,3},{3,2},{4,5},{5,4},{6,7},{7,6},{8,9},{9,8},{10,11... | collective-permute-start | bytes 3145736 | tf_op jit(solution)/shard_map/ppermute | solution.py:18
  163.0 14.9 %collective-permute-start.16 = (bf16[1,256,1024]{2,1,0:T(8,128)(2,1)S(1)}, bf16[1,256,1024]{2,1,0:T(8,128)(2,1)S(1)}, u32[]{:S(2)}, u32[]{:S(2)}) collective-permute-start(bf16[1,256,1024]{2,1,0:T(8,128)(2,1)S(1)} %get-tuple-element.60), channel_id=1, source_target_pairs={{0,2},{1,3},{2,0},{3,1},{4,6},{5,7},{6,4},{7,5},{8,10},{9,11},{10,... | collective-permute-start | bytes 1572872 | tf_op jit(solution)/shard_map/ppermute | solution.py:18
  164.9 24.1 %collective-permute-start.18 = (bf16[1,256,1024]{2,1,0:T(8,128)(2,1)S(1)}, bf16[1,256,1024]{2,1,0:T(8,128)(2,1)S(1)}, u32[]{:S(2)}, u32[]{:S(2)}) collective-permute-start(bf16[1,256,1024]{2,1,0:T(8,128)(2,1)S(1)} %get-tuple-element.64), channel_id=1, source_target_pairs={{0,2},{1,3},{2,0},{3,1},{4,6},{5,7},{6,4},{7,5},{8,10},{9,11},{10,... | collective-permute-start | bytes 1572872 | tf_op jit(solution)/shard_map/ppermute | solution.py:18
  165.9 34.4 %collective-permute-start.9 = (bf16[1,256,1024]{2,1,0:T(8,128)(2,1)S(1)}, bf16[1,256,1024]{2,1,0:T(8,128)(2,1)S(1)}, u32[]{:S(2)}, u32[]{:S(2)}) collective-permute-start(bf16[1,256,1024]{2,1,0:T(8,128)(2,1)S(1)} %get-tuple-element.52), channel_id=1, source_target_pairs={{0,2},{1,3},{2,0},{3,1},{4,6},{5,7},{6,4},{7,5},{8,10},{9,11},{10,... | collective-permute-start | bytes 1572872 | tf_op jit(solution)/shard_map/ppermute | solution.py:18
  167.5 43.2 %copy-start.5 = (bf16[4,128,2048]{2,1,0:T(8,128)(2,1)S(1)}, bf16[4,128,2048]{2,1,0:T(8,128)(2,1)}, u32[]{:S(2)}) copy-start(bf16[4,128,2048]{2,1,0:T(8,128)(2,1)} %param.26) | copy-start | bytes 6291460
  167.8 42.8 %collective-permute-start.7 = (bf16[1,256,1024]{2,1,0:T(8,128)(2,1)S(1)}, bf16[1,256,1024]{2,1,0:T(8,128)(2,1)S(1)}, u32[]{:S(2)}, u32[]{:S(2)}) collective-permute-start(bf16[1,256,1024]{2,1,0:T(8,128)(2,1)S(1)} %get-tuple-element.48), channel_id=1, source_target_pairs={{0,2},{1,3},{2,0},{3,1},{4,6},{5,7},{6,4},{7,5},{8,10},{9,11},{10,... | collective-permute-start | bytes 1572872 | tf_op jit(solution)/shard_map/ppermute | solution.py:18
